TPU v7x, 512 devices: a whole 4x4x16 slice. The times are simulated.
512 devices in a mesh: grp: 8 (over x, core), own: 64 (over z, y).
Axes of the slice: x: 4, y: 4, z: 16, core: 2. Of those that a mesh axis runs over, the one named last changes fastest.
Arguments:
- left: bfloat16 [32768, 128, 64], P(('grp', 'own')), may hold values from -0.75 to 0.75
- right: bfloat16 [32768, 128, 64], P(('grp', 'own')), may hold values from -0.75 to 0.75
- values: bfloat16 [32768, 128], P(('grp', 'own')), may hold values from -6 to 6
- core: bfloat16 [10240, 64, 64], P(('grp', 'own')), may hold values from -6 to 6
- tile_slice: int32 [32768], P(('grp', 'own')), may hold values from 0 to 10239, as said below
- tile_fill: int32 [32768], P(('grp', 'own')), may hold values from 64 to 128
Outputs:
- new_core: bfloat16 [10240, 64, 64], P(('grp', 'own'))
- new_left: bfloat16 [32768, 128, 64], P(('grp', 'own'))
Inputs may be any that keep to these rules, and one draw needn't show every extreme that they name: `tile_slice`: call j // 20 the block of slice j and its remainder mod 64 its class. Among the tiles of one device at most 2 have slices of one class; in every group of 64 consecutive devices some class gets exactly 2 tiles from every device of the group.
All inputs are finite; a program needn't handle non-finite values.
Results may differ from a plain program's by a relative error of at most 0.0052.
Values may be sent and summed in bfloat16 or wider, within the bound.
No kernel may reach another device: no remote copies, remote signals or barrier semaphores. Data moves between devices by JAX's collectives and lax.ppermute only.
A program may use at most 64 MiB of HBM per device.

v0:
```python
import jax
import jax.numpy as jnp
from jax import lax
from jax.sharding import PartitionSpec as P


def tile_terms(left_tiles, right_tiles, value_tiles, fill_counts, slice_tables):
    tile_rows = left_tiles.shape[1]
    projected = jnp.einsum(
        "sea,sab->seb", left_tiles, slice_tables, preferred_element_type=jnp.float32
    )
    predicted = jnp.sum(projected * right_tiles.astype(jnp.float32), axis=-1)
    live_rows = jnp.arange(tile_rows)[None, :] < fill_counts[:, None]
    residual = jnp.where(live_rows, predicted - value_tiles.astype(jnp.float32), 0.0)
    weighted = (residual[:, :, None] * left_tiles.astype(jnp.float32)).astype(jnp.bfloat16)
    return jnp.einsum("sea,seb->sab", weighted, right_tiles, preferred_element_type=jnp.float32)


def body(left, right, values, core, tile_slice, tile_fill):
    owners = lax.axis_size("own")
    groups = lax.axis_size("grp")
    tile_count, tile_rows, rank_width = left.shape
    per_device = core.shape[0]
    local_count = groups * per_device
    slot_cap = 2 * tile_count // owners
    slot_total = owners * slot_cap
    dev_block = tile_slice // per_device
    target_owner = dev_block % owners
    local_slice = dev_block // owners * per_device + tile_slice % per_device
    positions = jnp.arange(tile_count)
    same_owner = target_owner[:, None] == target_owner[None, :]
    earlier = positions[None, :] < positions[:, None]
    rank_among = jnp.sum((same_owner & earlier).astype(jnp.int32), axis=1)
    slot_of_tile = target_owner * slot_cap + rank_among
    slot_match = slot_of_tile[None, :] == jnp.arange(slot_total)[:, None]
    slot_live = jnp.any(slot_match, axis=1)
    tile_of_slot = jnp.sum(jnp.where(slot_match, positions[None, :], 0), axis=1)
    send_slice = jnp.where(slot_live, local_slice[tile_of_slot], 0)
    old_tables = lax.all_gather(core, "grp", axis=0, tiled=True)
    send_left = left[tile_of_slot]
    send_right = right[tile_of_slot]
    send_values = values[tile_of_slot]
    send_fill = jnp.where(slot_live, tile_fill[tile_of_slot], 0)
    got_left, got_right, got_values, got_slice, got_fill = (
        lax.all_to_all(send_left, "own", split_axis=0, concat_axis=0, tiled=True),
        lax.all_to_all(send_right, "own", split_axis=0, concat_axis=0, tiled=True),
        lax.all_to_all(send_values, "own", split_axis=0, concat_axis=0, tiled=True),
        lax.all_to_all(send_slice, "own", split_axis=0, concat_axis=0, tiled=True),
        lax.all_to_all(send_fill, "own", split_axis=0, concat_axis=0, tiled=True),
    )
    tile_grad = tile_terms(got_left, got_right, got_values, got_fill, old_tables[got_slice])
    selector = (got_slice[:, None] == jnp.arange(local_count)[None, :]).astype(jnp.float32)
    grad_part = jnp.dot(
        selector.T,
        tile_grad.reshape(slot_total, rank_width * rank_width),
        precision=lax.Precision.HIGHEST,
        preferred_element_type=jnp.float32,
    ).reshape(local_count, rank_width, rank_width)
    grad_whole = lax.psum(grad_part, "grp")
    new_tables = (old_tables.astype(jnp.float32) - grad_whole).astype(jnp.bfloat16)
    new_mine = lax.dynamic_slice_in_dim(
        new_tables, lax.axis_index("grp") * per_device, per_device, 0
    )
    refreshed = jnp.einsum(
        "sea,sab->seb", got_left, new_tables[got_slice], preferred_element_type=jnp.float32
    ).astype(jnp.bfloat16)
    returned = lax.all_to_all(refreshed, "own", split_axis=0, concat_axis=0, tiled=True)
    new_left = returned[slot_of_tile]
    return (new_mine, new_left)


def solution(mesh):
    return jax.shard_map(
        body,
        mesh=mesh,
        in_specs=(
            P(("grp", "own"), None, None),
            P(("grp", "own"), None, None),
            P(("grp", "own"), None),
            P(("grp", "own"), None, None),
            P(("grp", "own")),
            P(("grp", "own")),
        ),
        out_specs=(P(("grp", "own"), None, None), P(("grp", "own"), None, None)),
        check_vma=False,
    )
```

profile of v0, /device:TPU:7, one launch (start us, length us, event | category | flops | bytes accessed | tf_op | source)
XLA Modules:
  0.0 528.3 jit_solution(8652673713095691326)
XLA Ops:
  9.6 1.6 gather_fusion.1
  12.0 18.5 %all-to-all-start.1 = ((s32[64,2,1]{1,2,0:T(1,128)}), s32[64,2,1]{1,2,0:T(1,128)S(1)}, u32[]{:S(2)}, u32[]{:S(2)}) async-start(s32[64,2,1]{1,2,0:T(1,128)} %bitcast.4), calls=%async_computation.1 | async-start | bytes 65536 | tf_op jit(solution)/shard_map/all_to_all | solution.py:49
  31.2 12.7 %all-to-all-done.1 = s32[64,2,1]{1,2,0:T(1,128)S(1)} async-done(((s32[64,2,1]{1,2,0:T(1,128)}), s32[64,2,1]{1,2,0:T(1,128)S(1)}, u32[]{:S(2)}, u32[]{:S(2)}) %all-to-all-start.1) | async-done | bytes 544 | tf_op jit(solution)/shard_map/all_to_all | solution.py:49
  43.8 4.6 all-to-all-start
  48.4 2.1 gather_fusion.4
  50.6 11.4 %all-to-all-done = s32[64,2,1]{1,2,0:T(1,128)S(1)} async-done(((s32[64,2,1]{1,2,0:T(1,128)}), s32[64,2,1]{1,2,0:T(1,128)S(1)}, u32[]{:S(2)}, u32[]{:S(2)}) %all-to-all-start) | async-done | bytes 544 | tf_op jit(solution)/shard_map/all_to_all | solution.py:48
  61.9 4.7 all-to-all-start.3
  66.6 3.4 gather_fusion.2
  70.0 90.1 %all-to-all-done.3 = bf16[128,128,64]{1,2,0:T(8,128)(2,1)S(1)} async-done(((bf16[128,128,64]{1,2,0:T(8,128)(2,1)}), bf16[128,128,64]{1,2,0:T(8,128)(2,1)S(1)}, u32[]{:S(2)}, u32[]{:S(2)}) %all-to-all-start.3) | async-done | bytes 2097184 | tf_op jit(solution)/shard_map/all_to_all | solution.py:46
  160.2 1.3 copy-done.1
  161.5 10.7 %all-to-all-start.2 = ((bf16[128,128,64]{1,2,0:T(8,128)(2,1)}), bf16[128,128,64]{1,2,0:T(8,128)(2,1)S(1)}, u32[]{:S(2)}, u32[]{:S(2)}) async-start(bf16[128,128,64]{1,2,0:T(8,128)(2,1)} %gather_fusion.2), calls=%async_computation.2 | async-start | bytes 4194304 | tf_op jit(solution)/shard_map/all_to_all | solution.py:45
  172.9 1.3 gather_fusion.5
  176.7 34.6 %all-gather.2.cloned.1.call-done = bf16[160,64,64]{2,1,0:T(8,128)(2,1)} async-done(((bf16[20,64,64]{2,1,0:T(8,128)(2,1)}), bf16[160,64,64]{2,1,0:T(8,128)(2,1)}) %all-gather.2.cloned.1.call-update) | async-done | bytes 1310736 | tf_op jit(solution)/shard_map/all_gather | solution.py:39
  211.3 3.9 gather_fusion.3
  215.2 50.7 %all-to-all-done.2 = bf16[128,128,64]{1,2,0:T(8,128)(2,1)S(1)} async-done(((bf16[128,128,64]{1,2,0:T(8,128)(2,1)}), bf16[128,128,64]{1,2,0:T(8,128)(2,1)S(1)}, u32[]{:S(2)}, u32[]{:S(2)}) %all-to-all-start.2) | async-done | bytes 2097184 | tf_op jit(solution)/shard_map/all_to_all | solution.py:45
  265.9 11.0 %all-to-all-start.4 = ((bf16[64,2,128]{2,1,0:T(2,128)(2,1)}), bf16[64,2,128]{2,1,0:T(2,128)(2,1)S(1)}, u32[]{:S(2)}, u32[]{:S(2)}) async-start(bf16[64,2,128]{2,1,0:T(2,128)(2,1)} %bitcast.6), calls=%async_computation.4 | async-start | bytes 65536 | tf_op jit(solution)/shard_map/all_to_all | solution.py:47
  277.1 3.2 multiply_reduce_fusion
  280.4 9.9 %all-to-all-done.4 = bf16[64,2,128]{2,1,0:T(2,128)(2,1)S(1)} async-done(((bf16[64,2,128]{2,1,0:T(2,128)(2,1)}), bf16[64,2,128]{2,1,0:T(2,128)(2,1)S(1)}, u32[]{:S(2)}, u32[]{:S(2)}) %all-to-all-start.4) | async-done | bytes 32800 | tf_op jit(solution)/shard_map/all_to_all | solution.py:47
  290.4 4.8 fusion
  295.2 4.8 copy.30
  299.9 5.4 %fusion.1 = f32[160,64,64]{0,2,1:T(8,128)} fusion(f32[128,64,64]{0,2,1:T(8,128)} %copy.30, s32[128]{0:T(128)S(1)} %eq.50), kind=kOutput, calls=%fused_computation.12 | convolution fusion | flops 1006653440 | bytes 4719104 | tf_op jit(solution)/shard_map/dot_general | solution.py:53
  305.3 4.9 copy.26
  310.3 75.1 %all-reduce.2.cloned.1.call-done = f32[160,64,64]{0,2,1:T(8,128)} async-done(((f32[160,64,64]{0,2,1:T(8,128)}), f32[160,64,64]{0,2,1:T(8,128)}) %all-reduce.2.cloned.1.call-update) | async-done | bytes 2621456 | tf_op jit(solution)/shard_map/psum | solution.py:59
  385.4 5.0 subtract_convert_fusion
  390.4 5.0 copy.31
  395.4 3.9 gather_fusion.6
  399.3 3.8 convolution_convert_fusion
  403.0 15.8 %all-to-all-start.5 = ((bf16[128,128,64]{1,2,0:T(8,128)(2,1)}), bf16[128,128,64]{1,2,0:T(8,128)(2,1)}, u32[]{:S(2)}, u32[]{:S(2)}) async-start(bf16[128,128,64]{1,2,0:T(8,128)(2,1)} %convolution_convert_fusion), calls=%async_computation.5 | async-start | bytes 4194304 | tf_op jit(solution)/shard_map/all_to_all | solution.py:67
  418.8 1.5 constant_dynamic-slice_fusion
  420.3 2.6 copy.33
  422.8 95.4 %all-to-all-done.5 = bf16[128,128,64]{1,2,0:T(8,128)(2,1)} async-done(((bf16[128,128,64]{1,2,0:T(8,128)(2,1)}), bf16[128,128,64]{1,2,0:T(8,128)(2,1)}, u32[]{:S(2)}, u32[]{:S(2)}) %all-to-all-start.5) | async-done | bytes 2097184 | tf_op jit(solution)/shard_map/all_to_all | solution.py:67
  518.3 3.2 gather_fusion.7
  (33 shorter events, 7.4 us)
Async XLA Ops:
  7.2 41.3 %copy-start = (bf16[64,128,64]{1,2,0:T(8,128)(2,1)S(1)}, bf16[64,128,64]{1,2,0:T(8,128)(2,1)}, u32[]{:S(2)}) copy-start(bf16[64,128,64]{1,2,0:T(8,128)(2,1)} %param.7) | copy-start | bytes 3145732
  12.0 31.9 %all-to-all-start.1 = ((s32[64,2,1]{1,2,0:T(1,128)}), s32[64,2,1]{1,2,0:T(1,128)S(1)}, u32[]{:S(2)}, u32[]{:S(2)}) async-start(s32[64,2,1]{1,2,0:T(1,128)} %bitcast.4), calls=%async_computation.1 | async-start | bytes 65536 | tf_op jit(solution)/shard_map/all_to_all | solution.py:49
  43.8 18.1 %all-to-all-start = ((s32[64,2,1]{1,2,0:T(1,128)}), s32[64,2,1]{1,2,0:T(1,128)S(1)}, u32[]{:S(2)}, u32[]{:S(2)}) async-start(s32[64,2,1]{1,2,0:T(1,128)} %bitcast.2), calls=%async_computation | async-start | bytes 65536 | tf_op jit(solution)/shard_map/all_to_all | solution.py:48
  61.9 98.2 %all-to-all-start.3 = ((bf16[128,128,64]{1,2,0:T(8,128)(2,1)}), bf16[128,128,64]{1,2,0:T(8,128)(2,1)S(1)}, u32[]{:S(2)}, u32[]{:S(2)}) async-start(bf16[128,128,64]{1,2,0:T(8,128)(2,1)} %gather_fusion.4), calls=%async_computation.3 | async-start | bytes 4194304 | tf_op jit(solution)/shard_map/all_to_all | solution.py:46
  70.0 102.9 %copy-start.3 = (bf16[64,128]{1,0:T(8,128)(2,1)S(1)}, bf16[64,128]{1,0:T(8,128)(2,1)}, u32[]{:S(2)}) copy-start(bf16[64,128]{1,0:T(8,128)(2,1)} %param.8) | copy-start | bytes 49156
  160.2 1.3 copy-start.1
  161.5 104.4 %all-to-all-start.2 = ((bf16[128,128,64]{1,2,0:T(8,128)(2,1)}), bf16[128,128,64]{1,2,0:T(8,128)(2,1)S(1)}, u32[]{:S(2)}, u32[]{:S(2)}) async-start(bf16[128,128,64]{1,2,0:T(8,128)(2,1)} %gather_fusion.2), calls=%async_computation.2 | async-start | bytes 4194304 | tf_op jit(solution)/shard_map/all_to_all | solution.py:45
  172.2 39.1 %all-gather.2.cloned.1.call-start = ((), (), s32[]{:S(2)}) async-start(), calls=%async_computation.6 | async-start | bytes 2949120 | tf_op jit(solution)/shard_map/all_gather | solution.py:39
  265.9 24.4 %all-to-all-start.4 = ((bf16[64,2,128]{2,1,0:T(2,128)(2,1)}), bf16[64,2,128]{2,1,0:T(2,128)(2,1)S(1)}, u32[]{:S(2)}, u32[]{:S(2)}) async-start(bf16[64,2,128]{2,1,0:T(2,128)(2,1)} %bitcast.6), calls=%async_computation.4 | async-start | bytes 65536 | tf_op jit(solution)/shard_map/all_to_all | solution.py:47
  276.9 108.5 %all-reduce.2.cloned.1.call-start = ((), (), s32[]{:S(2)}) async-start(), calls=%async_computation.7 | async-start | bytes 8388608 | tf_op jit(solution)/shard_map/psum | solution.py:59
  403.0 15.8 %copy-start.2 = (bf16[160,64,64]{0,2,1:T(8,128)(2,1)S(1)}, bf16[160,64,64]{0,2,1:T(8,128)(2,1)}, u32[]{:S(2)}) copy-start(bf16[160,64,64]{0,2,1:T(8,128)(2,1)} %subtract_convert_fusion) | copy-start | bytes 3932164
  403.0 115.2 %all-to-all-start.5 = ((bf16[128,128,64]{1,2,0:T(8,128)(2,1)}), bf16[128,128,64]{1,2,0:T(8,128)(2,1)}, u32[]{:S(2)}, u32[]{:S(2)}) async-start(bf16[128,128,64]{1,2,0:T(8,128)(2,1)} %convolution_convert_fusion), calls=%async_computation.5 | async-start | bytes 4194304 | tf_op jit(solution)/shard_map/all_to_all | solution.py:67
Sparse Core Ops, SparseCore 0:
  175.1 36.1 all-gather.1
  305.5 79.8 all-reduce.1
where the time goes:
time: 529 us; the launch traced here: 528 us
  waiting for transfers between devices  381 us (72%)
  starting transfers between devices  65.5 us (12%)
  local copies, waits for them, and re-layouts  43.1 us (8%)
  matrix products  17.1 us (3%)
  between operations  14.2 us (3%)
  other arithmetic  7.74 us (1%)
    all_to_all x1, waiting for transfers between devices, body(): lax.all_to_all(refreshed, 'own', split_axis=0, concat_axis=0, tiled=True)  95.4 us
    all_to_all x1, waiting for transfers between devices, body(): lax.all_to_all(send_right, 'own', split_axis=0, concat_axis=0, tiled=True)  90.1 us
    psum x1, waiting for transfers between devices, body(): grad_whole = lax.psum(grad_part, 'grp')  75.1 us
    all_to_all x1, waiting for transfers between devices, body(): lax.all_to_all(send_left, 'own', split_axis=0, concat_axis=0, tiled=True)  50.7 us
    all_gather x1, waiting for transfers between devices, body(): old_tables = lax.all_gather(core, 'grp', axis=0, tiled=True)  34.6 us
    all_to_all x1, starting transfers between devices, body(): lax.all_to_all(send_fill, 'own', split_axis=0, concat_axis=0, tiled=True)  18.5 us
    all_to_all x1, starting transfers between devices, body(): lax.all_to_all(refreshed, 'own', split_axis=0, concat_axis=0, tiled=True)  15.8 us
    all_to_all x1, waiting for transfers between devices, body(): lax.all_to_all(send_fill, 'own', split_axis=0, concat_axis=0, tiled=True)  12.7 us
  transfers between devices with their start and end apart: 8, of which 8 were waited for; matrix products, arithmetic and copies ran while one was open for 5% of the time, Pallas kernels for 0%

commit v1 on v0

--- a/solution.py
+++ b/solution.py
@@ -2,6 +2,10 @@
 import jax.numpy as jnp
 from jax import lax
 from jax.sharding import PartitionSpec as P
+
+
+def arrays_play(inp):
+    return jnp.sum(lax.all_gather(inp, axis_name="grp"), 0)
 
 
 def tile_terms(left_tiles, right_tiles, value_tiles, fill_counts, slice_tables):
@@ -56,7 +60,7 @@
         precision=lax.Precision.HIGHEST,
         preferred_element_type=jnp.float32,
     ).reshape(local_count, rank_width, rank_width)
-    grad_whole = lax.psum(grad_part, "grp")
+    grad_whole = arrays_play(grad_part)
     new_tables = (old_tables.astype(jnp.float32) - grad_whole).astype(jnp.bfloat16)
     new_mine = lax.dynamic_slice_in_dim(
         new_tables, lax.axis_index("grp") * per_device, per_device, 0

time: 529 us -> 661 us (1.25)
  waiting for transfers between devices: 381 us -> 498 us
  other arithmetic: 7.74 us -> 26.9 us
  local copies, waits for them, and re-layouts: 43.1 us -> 33.1 us
    all_gather x0 -> x1, waiting for transfers between devices: none -> 191 us  [arrays_play(): return jnp.sum(lax.all_gather(inp, axis_name='grp'), 0)]
    psum x1 -> x0, waiting for transfers between devices: 75.1 us -> none  [body(): grad_whole = lax.psum(grad_part, 'grp')]
    all_to_all x1, waiting for transfers between devices: 50.7 us -> 91.4 us  [body(): lax.all_to_all(send_left, 'own', split_axis=0, concat_axis=0, tiled=True)]
    all_to_all x1, waiting for transfers between devices: 90.1 us -> 50.6 us  [body(): lax.all_to_all(send_right, 'own', split_axis=0, concat_axis=0, tiled=True)]
    reduce_sum x0 -> x1, other arithmetic: none -> 18.5 us  [arrays_play(): return jnp.sum(lax.all_gather(inp, axis_name='grp'), 0)]
    all_to_all x1, starting transfers between devices: 18.5 us -> 4.59 us  [body(): lax.all_to_all(send_fill, 'own', split_axis=0, concat_axis=0, tiled=True)]
    all_to_all x1, starting transfers between devices: 4.59 us -> 18.5 us  [body(): lax.all_to_all(send_slice, 'own', split_axis=0, concat_axis=0, tiled=True)]
  transfers between devices with their start and end apart: 8 -> 8, of which waited for: 8 -> 8; matrix products, arithmetic and copies ran while one was open for 5% -> 3% of each run, Pallas kernels for 0% -> 0%
where the time goes in v1:
time: 661 us; the launch traced here: 654 us
  waiting for transfers between devices  498 us (75%)
  starting transfers between devices  65.3 us (10%)
  local copies, waits for them, and re-layouts  33.1 us (5%)
  other arithmetic  26.9 us (4%)
  matrix products  17.1 us (3%)
  between operations  14.2 us (2%)
    all_gather x1, waiting for transfers between devices, arrays_play(): return jnp.sum(lax.all_gather(inp, axis_name='grp'), 0)  191 us
    all_to_all x1, waiting for transfers between devices, body(): lax.all_to_all(refreshed, 'own', split_axis=0, concat_axis=0, tiled=True)  95.2 us
    all_to_all x1, waiting for transfers between devices, body(): lax.all_to_all(send_left, 'own', split_axis=0, concat_axis=0, tiled=True)  91.4 us
    all_to_all x1, waiting for transfers between devices, body(): lax.all_to_all(send_right, 'own', split_axis=0, concat_axis=0, tiled=True)  50.6 us
    all_gather x1, waiting for transfers between devices, body(): old_tables = lax.all_gather(core, 'grp', axis=0, tiled=True)  34.6 us
    reduce_sum x1, other arithmetic, arrays_play(): return jnp.sum(lax.all_gather(inp, axis_name='grp'), 0)  18.5 us
    all_to_all x1, starting transfers between devices, body(): lax.all_to_all(send_slice, 'own', split_axis=0, concat_axis=0, tiled=True)  18.5 us
    all_to_all x1, starting transfers between devices, body(): lax.all_to_all(refreshed, 'own', split_axis=0, concat_axis=0, tiled=True)  15.4 us
  transfers between devices with their start and end apart: 8, of which 8 were waited for; matrix products, arithmetic and copies ran while one was open for 3% of the time, Pallas kernels for 0%

profile of v1, /device:TPU:7, one launch (start us, length us, event | category | flops | bytes accessed | tf_op | source)
XLA Modules:
  0.0 654.5 jit_solution(7932996817811939627)
XLA Ops:
  7.2 0.8 fusion.10
  8.4 1.2 gather_fusion
  9.6 1.6 gather_fusion.1
  12.0 18.5 %all-to-all-start = ((s32[64,2,1]{1,2,0:T(1,128)}), s32[64,2,1]{1,2,0:T(1,128)S(1)}, u32[]{:S(2)}, u32[]{:S(2)}) async-start(s32[64,2,1]{1,2,0:T(1,128)} %bitcast.2), calls=%async_computation | async-start | bytes 65536 | tf_op jit(solution)/shard_map/all_to_all | solution.py:52
  31.2 12.7 %all-to-all-done = s32[64,2,1]{1,2,0:T(1,128)S(1)} async-done(((s32[64,2,1]{1,2,0:T(1,128)}), s32[64,2,1]{1,2,0:T(1,128)S(1)}, u32[]{:S(2)}, u32[]{:S(2)}) %all-to-all-start) | async-done | bytes 544 | tf_op jit(solution)/shard_map/all_to_all | solution.py:52
  43.8 4.6 all-to-all-start.1
  48.4 2.1 gather_fusion.2
  50.6 11.4 %all-to-all-done.1 = s32[64,2,1]{1,2,0:T(1,128)S(1)} async-done(((s32[64,2,1]{1,2,0:T(1,128)}), s32[64,2,1]{1,2,0:T(1,128)S(1)}, u32[]{:S(2)}, u32[]{:S(2)}) %all-to-all-start.1) | async-done | bytes 544 | tf_op jit(solution)/shard_map/all_to_all | solution.py:53
  61.9 4.7 all-to-all-start.2
  66.7 2.1 gather_fusion.4
  68.8 91.4 %all-to-all-done.2 = bf16[128,128,64]{1,2,0:T(8,128)(2,1)S(1)} async-done(((bf16[128,128,64]{1,2,0:T(8,128)(2,1)}), bf16[128,128,64]{1,2,0:T(8,128)(2,1)S(1)}, u32[]{:S(2)}, u32[]{:S(2)}) %all-to-all-start.2) | async-done | bytes 2097184 | tf_op jit(solution)/shard_map/all_to_all | solution.py:49
  160.2 11.0 %all-to-all-start.3 = ((bf16[128,128,64]{1,2,0:T(8,128)(2,1)}), bf16[128,128,64]{1,2,0:T(8,128)(2,1)}, u32[]{:S(2)}, u32[]{:S(2)}) async-start(bf16[128,128,64]{1,2,0:T(8,128)(2,1)} %gather_fusion.4), calls=%async_computation.3 | async-start | bytes 4194304 | tf_op jit(solution)/shard_map/all_to_all | solution.py:50
  171.9 1.3 gather_fusion.5
  175.6 34.6 %all-gather.4.cloned.1.call-done = bf16[160,64,64]{2,1,0:T(8,128)(2,1)} async-done(((bf16[20,64,64]{2,1,0:T(8,128)(2,1)}), bf16[160,64,64]{2,1,0:T(8,128)(2,1)}) %all-gather.4.cloned.1.call-update) | async-done | bytes 1310736 | tf_op jit(solution)/shard_map/all_gather | solution.py:43
  210.2 3.9 gather_fusion.3
  214.0 50.6 %all-to-all-done.3 = bf16[128,128,64]{1,2,0:T(8,128)(2,1)} async-done(((bf16[128,128,64]{1,2,0:T(8,128)(2,1)}), bf16[128,128,64]{1,2,0:T(8,128)(2,1)}, u32[]{:S(2)}, u32[]{:S(2)}) %all-to-all-start.3) | async-done | bytes 2097184 | tf_op jit(solution)/shard_map/all_to_all | solution.py:50
  264.7 11.0 %all-to-all-start.4 = ((bf16[64,2,128]{2,1,0:T(2,128)(2,1)}), bf16[64,2,128]{2,1,0:T(2,128)(2,1)S(1)}, u32[]{:S(2)}, u32[]{:S(2)}) async-start(bf16[64,2,128]{2,1,0:T(2,128)(2,1)} %bitcast.6), calls=%async_computation.4 | async-start | bytes 65536 | tf_op jit(solution)/shard_map/all_to_all | solution.py:51
  275.9 3.2 multiply_reduce_fusion
  279.2 9.9 %all-to-all-done.4 = bf16[64,2,128]{2,1,0:T(2,128)(2,1)S(1)} async-done(((bf16[64,2,128]{2,1,0:T(2,128)(2,1)}), bf16[64,2,128]{2,1,0:T(2,128)(2,1)S(1)}, u32[]{:S(2)}, u32[]{:S(2)}) %all-to-all-start.4) | async-done | bytes 32800 | tf_op jit(solution)/shard_map/all_to_all | solution.py:51
  289.2 4.8 fusion
  293.9 4.8 copy.32
  298.7 5.3 fusion.1
  304.1 6.2 copy.33
  310.3 191.3 %all-gather.6.cloned.1.call-done = f32[1280,64,64]{2,1,0:T(8,128)} async-done(((f32[160,64,64]{2,1,0:T(8,128)}), f32[1280,64,64]{2,1,0:T(8,128)}) %all-gather.6.cloned.1.call-update) | async-done | bytes 20971536 | tf_op jit(solution)/shard_map/all_gather | solution.py:8
  501.6 18.5 %reduce_sum.42 = f32[160,64,64]{2,1,0:T(8,128)} reduce(f32[8,160,64,64]{3,2,1,0:T(8,128)} %bitcast.30, f32[]{:T(128)} %constant.58.clone.1), dimensions={0}, to_apply=%region_4.5 | reduce | flops 4587520 | bytes 23592964 | tf_op jit(solution)/shard_map/reduce_sum | solution.py:8
  520.2 5.7 subtract_convert_fusion
  525.9 3.9 gather_fusion.6
  529.8 3.8 convolution_convert_fusion
  533.6 15.4 %all-to-all-start.5 = ((bf16[128,128,64]{1,2,0:T(8,128)(2,1)}), bf16[128,128,64]{1,2,0:T(8,128)(2,1)S(1)}, u32[]{:S(2)}, u32[]{:S(2)}) async-start(bf16[128,128,64]{1,2,0:T(8,128)(2,1)} %convolution_convert_fusion), calls=%async_computation.5 | async-start | bytes 4194304 | tf_op jit(solution)/shard_map/all_to_all | solution.py:71
  549.0 1.8 constant_dynamic-slice_fusion
  550.8 95.2 %all-to-all-done.5 = bf16[128,128,64]{1,2,0:T(8,128)(2,1)S(1)} async-done(((bf16[128,128,64]{1,2,0:T(8,128)(2,1)}), bf16[128,128,64]{1,2,0:T(8,128)(2,1)S(1)}, u32[]{:S(2)}, u32[]{:S(2)}) %all-to-all-start.5) | async-done | bytes 2097184 | tf_op jit(solution)/shard_map/all_to_all | solution.py:71
  646.0 1.6 gather_fusion.7
  (32 shorter events, 5.4 us)
Async XLA Ops:
  7.2 41.3 %copy-start = (bf16[64,128,64]{1,2,0:T(8,128)(2,1)S(1)}, bf16[64,128,64]{1,2,0:T(8,128)(2,1)}, u32[]{:S(2)}) copy-start(bf16[64,128,64]{1,2,0:T(8,128)(2,1)} %param.6) | copy-start | bytes 3145732
  12.0 31.9 %all-to-all-start = ((s32[64,2,1]{1,2,0:T(1,128)}), s32[64,2,1]{1,2,0:T(1,128)S(1)}, u32[]{:S(2)}, u32[]{:S(2)}) async-start(s32[64,2,1]{1,2,0:T(1,128)} %bitcast.2), calls=%async_computation | async-start | bytes 65536 | tf_op jit(solution)/shard_map/all_to_all | solution.py:52
  43.8 18.1 %all-to-all-start.1 = ((s32[64,2,1]{1,2,0:T(1,128)}), s32[64,2,1]{1,2,0:T(1,128)S(1)}, u32[]{:S(2)}, u32[]{:S(2)}) async-start(s32[64,2,1]{1,2,0:T(1,128)} %bitcast.4), calls=%async_computation.1 | async-start | bytes 65536 | tf_op jit(solution)/shard_map/all_to_all | solution.py:53
  50.6 16.1 %copy-start.2 = (bf16[64,128,64]{1,2,0:T(8,128)(2,1)S(1)}, bf16[64,128,64]{1,2,0:T(8,128)(2,1)}, u32[]{:S(2)}) copy-start(bf16[64,128,64]{1,2,0:T(8,128)(2,1)} %param.7) | copy-start | bytes 3145732
  61.9 98.2 %all-to-all-start.2 = ((bf16[128,128,64]{1,2,0:T(8,128)(2,1)}), bf16[128,128,64]{1,2,0:T(8,128)(2,1)S(1)}, u32[]{:S(2)}, u32[]{:S(2)}) async-start(bf16[128,128,64]{1,2,0:T(8,128)(2,1)} %gather_fusion.2), calls=%async_computation.2 | async-start | bytes 4194304 | tf_op jit(solution)/shard_map/all_to_all | solution.py:49
  68.8 103.1 %copy-start.3 = (bf16[64,128]{1,0:T(8,128)(2,1)S(1)}, bf16[64,128]{1,0:T(8,128)(2,1)}, u32[]{:S(2)}) copy-start(bf16[64,128]{1,0:T(8,128)(2,1)} %param.8) | copy-start | bytes 49156
  160.2 104.5 %all-to-all-start.3 = ((bf16[128,128,64]{1,2,0:T(8,128)(2,1)}), bf16[128,128,64]{1,2,0:T(8,128)(2,1)}, u32[]{:S(2)}, u32[]{:S(2)}) async-start(bf16[128,128,64]{1,2,0:T(8,128)(2,1)} %gather_fusion.4), calls=%async_computation.3 | async-start | bytes 4194304 | tf_op jit(solution)/shard_map/all_to_all | solution.py:50
  171.1 39.0 %all-gather.4.cloned.1.call-start = ((), (), s32[]{:S(2)}) async-start(), calls=%async_computation.6 | async-start | bytes 2949120 | tf_op jit(solution)/shard_map/all_gather | solution.py:43
  264.7 24.4 %all-to-all-start.4 = ((bf16[64,2,128]{2,1,0:T(2,128)(2,1)}), bf16[64,2,128]{2,1,0:T(2,128)(2,1)S(1)}, u32[]{:S(2)}, u32[]{:S(2)}) async-start(bf16[64,2,128]{2,1,0:T(2,128)(2,1)} %bitcast.6), calls=%async_computation.4 | async-start | bytes 65536 | tf_op jit(solution)/shard_map/all_to_all | solution.py:51
  275.7 225.9 %all-gather.6.cloned.1.call-start = ((), (), s32[]{:S(2)}) async-start(), calls=%async_computation.7 | async-start | bytes 47185920 | tf_op jit(solution)/shard_map/all_gather | solution.py:8
  533.6 112.4 %all-to-all-start.5 = ((bf16[128,128,64]{1,2,0:T(8,128)(2,1)}), bf16[128,128,64]{1,2,0:T(8,128)(2,1)S(1)}, u32[]{:S(2)}, u32[]{:S(2)}) async-start(bf16[128,128,64]{1,2,0:T(8,128)(2,1)} %convolution_convert_fusion), calls=%async_computation.5 | async-start | bytes 4194304 | tf_op jit(solution)/shard_map/all_to_all | solution.py:71
  549.0 98.7 %copy-start.1 = (bf16[64,128,64]{1,2,0:T(8,128)(2,1)S(1)}, bf16[64,128,64]{1,2,0:T(8,128)(2,1)}, u32[]{:S(2)}) copy-start(bf16[64,128,64]{1,2,0:T(8,128)(2,1)} %param.6) | copy-start | bytes 3145732
Sparse Core Ops, SparseCore 0:
  174.1 36.0 all-gather.3
  310.4 191.1 all-gather.5
